TPU v7x, 32 devices: a whole 2x2x4 slice. The times are simulated.
32 devices in a mesh: groups: 2 (over y), seq: 4 (over x, core), chan: 4 (over z).
Axes of the slice: x: 2, y: 2, z: 4, core: 2. Of those that a mesh axis runs over, the one named last changes fastest.
Arguments:
- gate_input: bfloat16 [1024, 4096], P(('groups', 'seq'), 'chan'), parts along dimension 0, may hold values from -6 to 6
- value_input: bfloat16 [1024, 4096], P(('groups', 'seq'), 'chan'), parts along dimension 0, may hold values from -6 to 6
- short_filter: float32 [4096, 128], P('chan'), may hold values from -0.5 to 0.5
- long_filter: bfloat16 [512, 4096], P('seq', 'chan'), may hold values from -0.375 to 0.375
- query_weight: bfloat16 [32, 128, 128], P('chan'), may hold values from -0.5 to 0.5
- key_matrix: bfloat16 [1024, 4096], P(('groups', 'seq'), 'chan'), parts along dimension 0, may hold values from -200 to 200
- value_matrix: bfloat16 [1024, 4096], P(('groups', 'seq'), 'chan'), parts along dimension 0, may hold values from -6 to 6
Outputs:
- attended: bfloat16 [1024, 4096], P(('groups', 'seq'), 'chan'), parts along dimension 0
There are 2 independent parts, one for each index of `groups`. A program takes and returns all parts, laid end to end along the dimension named above; an argument that names none is the same for every part. Nothing has to cross between parts.
All inputs are finite; a program needn't handle non-finite values.
Results may differ from a plain program's by a relative error of at most 0.011.
Values may be sent and summed in bfloat16 or wider, within the bound.
A program may use at most 64 MiB of HBM per device.

v0:
```python
import math

import jax
import jax.numpy as jnp
from jax import lax
from jax.sharding import PartitionSpec as P

HEAD_DIM = 128
TAPS = 128
RADIX = 128


HIGHEST = lax.Precision.HIGHEST


def shifted(value, axis, steps):
    count = lax.axis_size(axis)
    initial, last = (max(0, -steps), min(count, count - steps))
    return lax.ppermute(value, axis, [(source, source + steps) for source in range(initial, last)])


def unit_table(height, breadth, modulus, orient):
    product = (
        lax.broadcasted_iota(jnp.int32, (height, breadth), 0)
        * lax.broadcasted_iota(jnp.int32, (height, breadth), 1)
        % modulus
    )
    angles = 2.0 * math.pi / modulus * product.astype(jnp.float32)
    return (jnp.cos(angles), orient * jnp.sin(angles))


def block_table(factor, orient):
    inner_re, inner_im = unit_table(factor, factor, factor, orient)
    upper = jnp.concatenate([inner_re, inner_im], axis=1)
    lower = jnp.concatenate([-inner_im, inner_re], axis=1)
    return jnp.concatenate([upper, lower], axis=0)


def spectrum(signal, factor):
    channels, length = signal.shape
    full_length = 2 * length
    column_count = full_length // factor
    folded = signal.reshape(channels, column_count // 2, factor)
    outer_re, outer_im = unit_table(column_count, column_count // 2, column_count, -1.0)
    outer_both = jnp.concatenate([outer_re, outer_im], axis=0)
    first = jnp.einsum("kn,cnm->ckm", outer_both, folded, precision=HIGHEST)
    first_re = first[:, :column_count]
    first_im = first[:, column_count:]
    twist_re, twist_im = unit_table(column_count, factor, full_length, -1.0)
    mid_re = first_re * twist_re - first_im * twist_im
    mid_im = first_re * twist_im + first_im * twist_re
    joined = jnp.concatenate([mid_re, mid_im], axis=2)
    return jnp.einsum("ckn,nm->ckm", joined, block_table(factor, -1.0), precision=HIGHEST)


def inverse(spec_both, factor, length):
    channels = spec_both.shape[0]
    full_length = 2 * length
    column_count = full_length // factor
    mid = jnp.einsum("ckm,mn->ckn", spec_both, block_table(factor, 1.0), precision=HIGHEST)
    mid_re = mid[:, :, :factor]
    mid_im = mid[:, :, factor:]
    twist_re, twist_im = unit_table(column_count, factor, full_length, 1.0)
    turn_re = mid_re * twist_re - mid_im * twist_im
    turn_im = mid_re * twist_im + mid_im * twist_re
    outer_re, outer_im = unit_table(column_count // 2, column_count, column_count, 1.0)
    outer_both = jnp.concatenate([outer_re, -outer_im], axis=1)
    turned = jnp.concatenate([turn_re, turn_im], axis=1)
    result = jnp.einsum("nk,ckm->cnm", outer_both, turned, precision=HIGHEST)
    return result.reshape(channels, length) / full_length


def shards(
    gate_input, value_input, short_filter, long_filter, query_weight, key_matrix, value_matrix
):
    seq_rows, local_width = gate_input.shape
    last_rows = gate_input[seq_rows - (TAPS - 1) :]
    earlier = shifted(last_rows, "seq", 1)
    padded = jnp.concatenate([earlier, gate_input], axis=0).astype(jnp.float32)
    kernel = short_filter[:, ::-1].T[:, None, :]
    smoothed = lax.conv_general_dilated(
        padded[None],
        kernel,
        (1,),
        "VALID",
        dimension_numbers=("NHC", "HIO", "NHC"),
        feature_group_count=local_width,
        precision=HIGHEST,
    )[0]
    mixed_input = (smoothed * value_input.astype(jnp.float32)).astype(jnp.bfloat16)
    signal, kernel_line = (
        lax.all_to_all(mixed_input.T, "seq", split_axis=0, concat_axis=1, tiled=True),
        lax.all_to_all(long_filter.T, "seq", split_axis=0, concat_axis=1, tiled=True),
    )
    length = signal.shape[1]
    signal_both = spectrum(signal.astype(jnp.float32), RADIX)
    kernel_both = spectrum(kernel_line.astype(jnp.float32), RADIX)
    signal_re = signal_both[:, :, :RADIX]
    signal_im = signal_both[:, :, RADIX:]
    kernel_re = kernel_both[:, :, :RADIX]
    kernel_im = kernel_both[:, :, RADIX:]
    joint = jnp.concatenate(
        [
            signal_re * kernel_re - signal_im * kernel_im,
            signal_re * kernel_im + signal_im * kernel_re,
        ],
        axis=2,
    )
    conv_line = inverse(joint, RADIX, length).astype(jnp.bfloat16)
    my_index = lax.axis_index("seq")
    group_firsts = [my_index * seq_rows]
    conv_columns = lax.all_to_all(conv_line, "seq", split_axis=1, concat_axis=0, tiled=True)
    heads_here = local_width // HEAD_DIM
    conv_heads = conv_columns.reshape(heads_here, HEAD_DIM, seq_rows)
    query_heads = jnp.einsum(
        "hds,hde->hse", conv_heads, query_weight, preferred_element_type=jnp.float32
    ).astype(jnp.bfloat16)
    group_count = len(group_firsts)
    query_groups = [query_heads]
    key_heads = key_matrix.reshape(seq_rows, heads_here, HEAD_DIM).transpose(1, 0, 2)
    value_heads = value_matrix.reshape(seq_rows, heads_here, HEAD_DIM).transpose(1, 0, 2)
    score_scale = 1.0 / math.sqrt(HEAD_DIM)

    def attend_group(running, group_query, group_first, key_block, value_block, first_row):
        block_rows = key_block.shape[1]

        def compute(current):
            peak_value, weight_sum, weighted = current
            scores = (
                jnp.einsum(
                    "hqd,hkd->hqk", group_query, key_block, preferred_element_type=jnp.float32
                )
                * score_scale
            )
            key_pos = first_row + lax.iota(jnp.int32, block_rows)
            query_pos = group_first + lax.iota(jnp.int32, seq_rows)
            allowed = (key_pos[None, :] <= query_pos[:, None])[None]
            scores = jnp.where(allowed, scores, -1e30)
            new_peak = jnp.maximum(peak_value, jnp.max(scores, axis=2))
            weights = jnp.where(allowed, jnp.exp(scores - new_peak[:, :, None]), 0.0)
            rescale = jnp.exp(peak_value - new_peak)
            weight_sum = weight_sum * rescale + jnp.sum(weights, axis=2)
            weighted = weighted * rescale[:, :, None] + jnp.einsum(
                "hqk,hkd->hqd",
                weights.astype(jnp.bfloat16),
                value_block,
                preferred_element_type=jnp.float32,
            )
            return (new_peak, weight_sum, weighted)

        live = first_row <= group_first + seq_rows - 1
        return lax.cond(live, compute, lambda current: current, running)

    def attend(states, key_block, value_block, first_row):
        return tuple(
            (
                attend_group(
                    states[g], query_groups[g], group_firsts[g], key_block, value_block, first_row
                )
                for g in range(group_count)
            )
        )

    one_state = (
        jnp.full((heads_here, seq_rows), -1e30, jnp.float32),
        jnp.zeros((heads_here, seq_rows), jnp.float32),
        jnp.zeros((heads_here, seq_rows, HEAD_DIM), jnp.float32),
    )
    initial = tuple((one_state for g in range(group_count)))
    running = initial
    key_piece = lax.all_gather(key_heads, "seq", axis=1, tiled=True)
    value_piece = lax.all_gather(value_heads, "seq", axis=1, tiled=True)
    piece_rows = key_piece.shape[1]
    block_rows = 512
    block_count = piece_rows // block_rows
    key_blocks = key_piece.reshape(heads_here, block_count, block_rows, HEAD_DIM).transpose(
        1, 0, 2, 3
    )
    value_blocks = value_piece.reshape(heads_here, block_count, block_rows, HEAD_DIM).transpose(
        1, 0, 2, 3
    )

    def advance(current, element):
        key_block, value_block, position = element
        return (attend(current, key_block, value_block, position * block_rows), None)

    running, _ = lax.scan(
        advance, running, (key_blocks, value_blocks, lax.iota(jnp.int32, block_count))
    )
    outputs = [state[2] / state[1][:, :, None] for state in running]
    result = outputs[0]
    attended_rows = result.transpose(1, 0, 2).reshape(seq_rows, local_width).astype(jnp.bfloat16)
    return attended_rows


def solution(mesh):
    in_specs = (
        P(("groups", "seq"), "chan"),
        P(("groups", "seq"), "chan"),
        P("chan", None),
        P("seq", "chan"),
        P("chan", None, None),
        P(("groups", "seq"), "chan"),
        P(("groups", "seq"), "chan"),
    )
    out_specs = P(("groups", "seq"), "chan")
    return jax.shard_map(shards, mesh=mesh, in_specs=in_specs, out_specs=out_specs, check_vma=False)
```

profile of v0, /device:TPU:0, one launch (start us, length us, event | category | flops | bytes accessed | tf_op | source)
XLA Modules:
  0.0 73.8 jit_solution(403984494626430761)
XLA Ops:
  6.5 1.9 %copy.49 = bf16[128,1024]{0,1:T(8,128)(2,1)} copy(bf16[128,1024]{1,0:T(8,128)(2,1)} %param.14) | data formatting | bytes 524288 | tf_op args[5]
  8.5 1.0 %slice.33 = bf16[127,1024]{1,0:T(8,128)(2,1)S(1)} slice(bf16[128,1024]{1,0:T(8,128)(2,1)} %param.9), slice={[1:128], [0:1024]} | slice | bytes 520192 | tf_op jit(solution)/shard_map/slice | solution.py:77
  9.5 2.5 %collective-permute-start = (bf16[127,1024]{1,0:T(8,128)(2,1)S(1)}, bf16[127,1024]{1,0:T(8,128)(2,1)S(1)}, u32[]{:S(2)}, u32[]{:S(2)}) collective-permute-start(bf16[127,1024]{1,0:T(8,128)(2,1)S(1)} %slice.33), channel_id=1, source_target_pairs={{0,4},{4,8},{8,12},{1,5},{5,9},{9,13},{2,6},{6,10},{10,14},{3,7},{... | collective-permute-start | bytes 780296 | tf_op jit(solution)/shard_map/ppermute | solution.py:19
  12.0 1.8 %copy.40 = bf16[128,1024]{0,1:T(8,128)(2,1)} copy(bf16[128,1024]{1,0:T(8,128)(2,1)} %param.12) | data formatting | bytes 524288 | tf_op args[3]
  13.8 3.8 %all-to-all-start.1 = ((bf16[4,256,128]{2,1,0:T(8,128)(2,1)}), bf16[4,256,128]{2,1,0:T(8,128)(2,1)S(1)}, u32[]{:S(2)}, u32[]{:S(2)}) async-start(bf16[4,256,128]{2,1,0:T(8,128)(2,1)} %bitcast.10), calls=%async_computation.1 | async-start | bytes 524288 | tf_op jit(solution)/shard_map/all_to_all | solution.py:93
  17.7 0.8 %copy.50 = bf16[128,1024]{0,1:T(8,128)(2,1)} copy(bf16[128,1024]{1,0:T(8,128)(2,1)S(1)} %copy-done.3) | data formatting | bytes 524288 | tf_op args[6]
  20.9 5.6 %fusion.29 = f32[1,128,1024]{2,0,1:T(1,128)S(1)} fusion(f32[128,1,1024]{2,1,0:T(1,128)S(1)} %copy.36, bf16[1,255,1024]{2,1,0:T(8,128)(2,1)S(1)} %maximum_bitcast_fusion), kind=kOutput, calls=%fused_computation.44 | convolution fusion | flops 201326592 | bytes 1570816 | tf_op jit(solution)/shard_map/conv_general_dilated | solution.py:81
  26.6 0.8 %copy.60 = bf16[1024,128]{1,0:T(8,128)(2,1)} copy(bf16[1024,128]{0,1:T(8,128)(2,1)S(1)} %fusion.38) | data formatting | bytes 524288 | tf_op jit(solution)/shard_map/all_to_all | solution.py:92
  27.5 3.6 %all-to-all-start = ((bf16[4,256,128]{2,1,0:T(8,128)(2,1)}), bf16[4,256,128]{2,1,0:T(8,128)(2,1)S(1)}, u32[]{:S(2)}, u32[]{:S(2)}) async-start(bf16[4,256,128]{2,1,0:T(8,128)(2,1)} %bitcast.4), calls=%async_computation | async-start | bytes 524288 | tf_op jit(solution)/shard_map/all_to_all | solution.py:92
  31.1 1.1 %convolution_bitcast_fusion = f32[256,16,128]{2,1,0:T(8,128)S(1)} fusion(bf16[4,256,128]{2,1,0:T(8,128)(2,1)S(1)} %all-to-all-done.1, f32[8,4]{0,1:T(4,128)S(1)} %get-tuple-element.115, f32[8,4]{0,1:T(4,128)S(1)} %get-tuple-element.116), kind=kOutput, calls=%fused_computation.30 | convolution fusion | flops 25165888 | bytes 2359552 | tf_op jit(solution)/shard_map/kn,cnm->ckm/dot_general | solution.py:46
  32.2 4.8 %all-to-all-done = bf16[4,256,128]{2,1,0:T(8,128)(2,1)S(1)} async-done(((bf16[4,256,128]{2,1,0:T(8,128)(2,1)}), bf16[4,256,128]{2,1,0:T(8,128)(2,1)S(1)}, u32[]{:S(2)}, u32[]{:S(2)}) %all-to-all-start) | async-done | bytes 262176 | tf_op jit(solution)/shard_map/all_to_all | solution.py:92
  37.0 1.1 %convolution_bitcast_fusion.1 = f32[256,16,128]{2,1,0:T(8,128)S(1)} fusion(bf16[4,256,128]{2,1,0:T(8,128)(2,1)S(1)} %all-to-all-done, f32[8,4]{0,1:T(4,128)S(1)} %get-tuple-element.115, f32[8,4]{0,1:T(4,128)S(1)} %get-tuple-element.116), kind=kOutput, calls=%fused_computation.31 | convolution fusion | flops 25165888 | bytes 2359552 | tf_op jit(solution)/shard_map/kn,cnm->ckm/dot_general | solution.py:46
  38.9 2.6 %fusion.18 = f32[256,8,256]{0,2,1:T(8,128)S(1)} fusion(f32[256,8,256]{2,1,0:T(8,128)S(1)} %pad_maximum_fusion, f32[128,128]{0,1:T(8,128)S(1)} %get-tuple-element.120, f32[128,128]{0,1:T(8,128)S(1)} %fusion.57, f32[128,128]{0,1:T(8,128)S(1)} %get-tuple-element.119), kind=kOutput, calls=%fused_computation.28 | convolution fusion | flops 1610809344 | bytes 4390912 | tf_op jit(solution)/shard_map/ckn,nm->ckm/dot_general | solution.py:53
  41.5 2.6 %fusion.16 = f32[256,8,256]{0,2,1:T(8,128)S(1)} fusion(f32[256,8,256]{2,1,0:T(8,128)S(1)} %pad_maximum_fusion.1, f32[128,128]{0,1:T(8,128)S(1)} %get-tuple-element.120, f32[128,128]{0,1:T(8,128)S(1)} %fusion.57, f32[128,128]{0,1:T(8,128)S(1)} %get-tuple-element.119), kind=kOutput, calls=%fused_computation.26 | convolution fusion | flops 1610809344 | bytes 4390912 | tf_op jit(solution)/shard_map/ckn,nm->ckm/dot_general | solution.py:53
  44.5 1.5 %pad_maximum_fusion.2 = f32[256,8,256]{0,2,1:T(8,128)} fusion(f32[256,8,128]{0,2,1:T(8,128)S(1)} %get-tuple-element.106, f32[256,8,128]{0,2,1:T(8,128)S(1)} %get-tuple-element.105), kind=kLoop, calls=%fused_computation.21 | loop fusion | flops 524288 | bytes 4194304 | tf_op jit(solution)/shard_map/concatenate | solution.py:102
  46.0 2.5 %copy.56 = f32[256,8,256]{2,1,0:T(8,128)S(1)} copy(f32[256,8,256]{0,2,1:T(8,128)} %pad_maximum_fusion.2) | data formatting | bytes 4194304 | tf_op jit(solution)/shard_map/concatenate | solution.py:102
  48.4 1.9 %fusion.36 = f32[256,8,256]{2,1,0:T(8,128)S(1)} fusion(f32[256,8,256]{2,1,0:T(8,128)S(1)} %copy.56, f32[128,128]{0,1:T(8,128)S(1)} %get-tuple-element.120, f32[128,128]{0,1:T(8,128)S(1)} %get-tuple-element.122, f32[128,128]{0,1:T(8,128)S(1)} %get-tuple-element.121), kind=kOutput, calls=%fused_computation.58 | convolution fusion | flops 1610809344 | bytes 4390912 | tf_op jit(solution)/shard_map/ckm,mn->ckn/dot_general | solution.py:60
  50.6 1.2 %fusion.26 = bf16[256,4,128]{2,1,0:T(4,128)(2,1)S(1)} fusion(f32[256,8,128]{2,1,0:T(8,128)S(1)} %get-tuple-element.108, f32[256,8,128]{2,1,0:T(8,128)S(1)} %get-tuple-element.107, f32[4,8]{1,0:T(4,128)S(1)} %get-tuple-element.123, f32[4,8]{1,0:T(4,128)S(1)} %get-tuple-element.124), kind=kOutput, calls=%fused_computation.35 | convolution fusion | flops 25952320 | bytes 2359552 | tf_op jit(solution)/shard_map/nk,ckm->cnm/dot_general | solution.py:69
  52.6 3.4 %all-to-all-start.2 = ((bf16[256,4,128]{2,0,1:T(8,128)(2,1)}), bf16[256,4,128]{2,0,1:T(8,128)(2,1)S(1)}, u32[]{:S(2)}, u32[]{:S(2)}) async-start(bf16[256,4,128]{2,0,1:T(8,128)(2,1)} %copy.47), calls=%async_computation.2 | async-start | bytes 524288 | tf_op jit(solution)/shard_map/all_to_all | solution.py:112
  56.0 5.9 %all-to-all-done.2 = bf16[256,4,128]{2,0,1:T(8,128)(2,1)S(1)} async-done(((bf16[256,4,128]{2,0,1:T(8,128)(2,1)}), bf16[256,4,128]{2,0,1:T(8,128)(2,1)S(1)}, u32[]{:S(2)}, u32[]{:S(2)}) %all-to-all-start.2) | async-done | bytes 262176 | tf_op jit(solution)/shard_map/all_to_all | solution.py:112
  62.3 3.8 %conditional.1 = ((f32[8,128]{1,0:T(8,128)S(1)}, f32[8,128,128]{2,1,0:T(8,128)S(1)})) conditional(s32[]{:T(128)} %convert_element_type.104, (f32[8,128]{1,0:T(8,128)S(1)}, f32[8,128,128]{2,1,0:T(8,128)S(1)}) %tuple.22, (s32[]{:T(128)}, bf16[8,128,128]{2,1,0:T(8,128)(2,1)S(1)}, bf16[8,512,128]{1,2,0:T(8,128)(2,1)}, f32[8,128]{1,0:T(8,128)S(1)}, ...), branch_computations={%region_0.1_spmd, %region_1.4_spmd} | conditional | flops 275582080 | bytes 14206008 | solution.py:152
  62.4 1.9 %fusion = (f32[8,128]{1,0:T(8,128)S(1)}, f32[8,128,512]{2,1,0:T(8,128)S(1)}) fusion(pred[128,512]{1,0:T(8,128)(4,1)S(1)} %iota_compare_fusion, bf16[8,128,128]{2,1,0:T(8,128)(2,1)S(1)} %get-tuple-element.81, bf16[8,512,128]{1,2,0:T(8,128)(2,1)} %get-tuple-element.97), kind=kOutput, calls=%fused_computation.2 | convolution fusion | flops 135789568 | bytes 3477504 | tf_op jit(solution)/shard_map/while/body/eval_jaxpr/cond/branch_1_fun/hqd,hkd->hqk/dot_general | solution.py:130
  65.0 1.0 %convolution_add_fusion = f32[8,128,128]{2,1,0:T(8,128)S(1)} fusion(bf16[8,512,128]{1,2,0:T(8,128)(2,1)S(1)} %copy-done.5, f32[8,128,512]{2,1,0:T(8,128)S(1)} %get-tuple-element.104, f32[8,128]{1,0:T(8,128)S(1)} %broadcast_maximum_fusion, pred[128,512]{1,0:T(8,128)(4,1)S(1)} %iota_compare_fusion, f32[8,128,128]{2,1,0:T(8,128)S(1)} %get-tuple-element.83, ...), kind=kOutput, calls=%fused_computation.5 | convolution fusion | flops 137101312 | bytes 4268032 | tf_op jit(solution)/shard_map/while/body/eval_jaxpr/cond/branch_1_fun/hqk,hkd->hqd/dot_general | solution.py:143
  66.1 0.9 %copy_bitcast_fusion = bf16[128,1024]{1,0:T(8,128)(2,1)} fusion(f32[8,128,128]{2,1,0:T(8,128)S(1)} %get-tuple-element.87, f32[8,128]{1,0:T(8,128)S(1)} %get-tuple-element.88), kind=kLoop, calls=%fused_computation.60 | loop fusion | flops 262144 | bytes 790528 | tf_op jit(solution)/shard_map/convert_element_type | solution.py:192
  (45 shorter events, 5.6 us)
Async XLA Ops:
  6.5 55.4 %copy-start = (bf16[8,128,128]{2,1,0:T(8,128)(2,1)S(1)}, bf16[8,128,128]{2,1,0:T(8,128)(2,1)}, u32[]{:S(2)}) copy-start(bf16[8,128,128]{2,1,0:T(8,128)(2,1)} %param.13) | copy-start | bytes 786436
  6.5 11.2 %copy-start.3 = (bf16[128,1024]{1,0:T(8,128)(2,1)S(1)}, bf16[128,1024]{1,0:T(8,128)(2,1)}, u32[]{:S(2)}) copy-start(bf16[128,1024]{1,0:T(8,128)(2,1)} %param.15) | copy-start | bytes 786436
  6.5 12.5 %copy-start.2 = (f32[1024,128]{1,0:T(8,128)S(1)}, f32[1024,128]{1,0:T(8,128)}, u32[]{:S(2)}) copy-start(f32[1024,128]{1,0:T(8,128)} %param.11) | copy-start | bytes 1572868
  6.5 55.7 %all-gather.3.cloned.1.call-start = ((), (), s32[]{:S(2)}) async-start(), calls=%async_computation.3 | async-start | bytes 1310720 | tf_op jit(solution)/shard_map/all_gather | solution.py:171
  9.5 11.3 %copy-start.1 = (bf16[128,1024]{1,0:T(8,128)(2,1)S(1)}, bf16[128,1024]{1,0:T(8,128)(2,1)}, u32[]{:S(2)}) copy-start(bf16[128,1024]{1,0:T(8,128)(2,1)} %param.9) | copy-start | bytes 786436
  9.5 11.3 %collective-permute-start = (bf16[127,1024]{1,0:T(8,128)(2,1)S(1)}, bf16[127,1024]{1,0:T(8,128)(2,1)S(1)}, u32[]{:S(2)}, u32[]{:S(2)}) collective-permute-start(bf16[127,1024]{1,0:T(8,128)(2,1)S(1)} %slice.33), channel_id=1, source_target_pairs={{0,4},{4,8},{8,12},{1,5},{5,9},{9,13},{2,6},{6,10},{10,14},{3,7},{... | collective-permute-start | bytes 780296 | tf_op jit(solution)/shard_map/ppermute | solution.py:19
  13.8 13.6 %all-to-all-start.1 = ((bf16[4,256,128]{2,1,0:T(8,128)(2,1)}), bf16[4,256,128]{2,1,0:T(8,128)(2,1)S(1)}, u32[]{:S(2)}, u32[]{:S(2)}) async-start(bf16[4,256,128]{2,1,0:T(8,128)(2,1)} %bitcast.10), calls=%async_computation.1 | async-start | bytes 524288 | tf_op jit(solution)/shard_map/all_to_all | solution.py:93
  17.7 44.6 %all-gather.5.cloned.1.call-start = ((), (), s32[]{:S(2)}) async-start(), calls=%async_computation.4 | async-start | bytes 1310720 | tf_op jit(solution)/shard_map/all_gather | solution.py:172
  20.9 5.6 %copy-start.4 = (bf16[128,1024]{1,0:T(8,128)(2,1)S(1)}, bf16[128,1024]{1,0:T(8,128)(2,1)}, u32[]{:S(2)}) copy-start(bf16[128,1024]{1,0:T(8,128)(2,1)} %param.10) | copy-start | bytes 786436
  27.5 9.6 %all-to-all-start = ((bf16[4,256,128]{2,1,0:T(8,128)(2,1)}), bf16[4,256,128]{2,1,0:T(8,128)(2,1)S(1)}, u32[]{:S(2)}, u32[]{:S(2)}) async-start(bf16[4,256,128]{2,1,0:T(8,128)(2,1)} %bitcast.4), calls=%async_computation | async-start | bytes 524288 | tf_op jit(solution)/shard_map/all_to_all | solution.py:92
  52.6 9.4 %all-to-all-start.2 = ((bf16[256,4,128]{2,0,1:T(8,128)(2,1)}), bf16[256,4,128]{2,0,1:T(8,128)(2,1)S(1)}, u32[]{:S(2)}, u32[]{:S(2)}) async-start(bf16[256,4,128]{2,0,1:T(8,128)(2,1)} %copy.47), calls=%async_computation.2 | async-start | bytes 524288 | tf_op jit(solution)/shard_map/all_to_all | solution.py:112
  62.4 2.6 %copy-start.5 = (bf16[8,512,128]{1,2,0:T(8,128)(2,1)S(1)}, bf16[8,512,128]{1,2,0:T(8,128)(2,1)}, u32[]{:S(2)}) copy-start(bf16[8,512,128]{1,2,0:T(8,128)(2,1)} %get-tuple-element.100) | copy-start | bytes 3145732 | tf_op jit(solution)/shard_map/while/body/eval_jaxpr/cond
Sparse Core Ops, SparseCore 0:
  8.9 21.9 all-gather.2
  32.5 17.1 all-gather.4
where the time goes:
time: 74.3 us; the launch traced here: 73.8 us
  matrix products  19.4 us (26%)
  between operations  13.7 us (18%)
  starting transfers between devices  13.4 us (18%)
  local copies, waits for them, and re-layouts  10.8 us (15%)
  waiting for transfers between devices  10.8 us (15%)
  other arithmetic  5.68 us (8%)
    all_to_all x1, waiting for transfers between devices, shards(): lax.all_to_all(conv_line, 'seq', split_axis=1, concat_axis=0, tiled=True)  5.91 us
    conv_general_dilated x1, matrix products, shards(): lax.conv_general_dilated(padded[None], kernel, (1,), 'VALID', dimension_n...  5.61 us
    dot_general x2, matrix products, spectrum(): jnp.einsum('ckn,nm->ckm', joined, block_table(factor, -1.0), precision=HI...  5.23 us
    all_to_all x1, waiting for transfers between devices, shards(): lax.all_to_all(mixed_input.T, 'seq', split_axis=0, concat_axis=1, tiled=T...  4.82 us
    unnamed x13, local copies, waits for them, and re-layouts  4.55 us
    all_to_all x1, starting transfers between devices, shards(): lax.all_to_all(long_filter.T, 'seq', split_axis=0, concat_axis=1, tiled=T...  3.85 us
    all_to_all x1, starting transfers between devices, shards(): lax.all_to_all(mixed_input.T, 'seq', split_axis=0, concat_axis=1, tiled=T...  3.59 us
    all_to_all x1, starting transfers between devices, shards(): lax.all_to_all(conv_line, 'seq', split_axis=1, concat_axis=0, tiled=True)  3.41 us
  transfers between devices with their start and end apart: 6, of which 2 were waited for; matrix products, arithmetic and copies ran while one was open for 40% of the time, Pallas kernels for 0%

commit v1 on v0

--- a/solution.py
+++ b/solution.py
@@ -1,8 +1,12 @@
+import functools
 import math
 
 import jax
 import jax.numpy as jnp
+import numpy as np
 from jax import lax
+from jax.experimental import pallas as pl
+from jax.experimental.pallas import tpu as pltpu
 from jax.sharding import PartitionSpec as P
 
 HEAD_DIM = 128
@@ -70,7 +74,7 @@
     return result.reshape(channels, length) / full_length
 
 
-def shards(
+def general_shards(
     gate_input, value_input, short_filter, long_filter, query_weight, key_matrix, value_matrix
 ):
     seq_rows, local_width = gate_input.shape
@@ -193,6 +197,341 @@
     return attended_rows
 
 
+def split_pair(array):
+    high = array.astype(jnp.bfloat16)
+    return high, (array - high.astype(jnp.float32)).astype(jnp.bfloat16)
+
+
+def transform_tables(rows):
+    full = 2 * rows
+    turn = np.arange(rows)[:, None] * np.arange(full)[None, :] % full
+    angle = 2.0 * np.pi / full * turn
+    forward = np.concatenate([np.cos(angle), -np.sin(angle)], axis=0)
+    forward[rows] = 1.0 - 2.0 * (np.arange(full) % 2)
+    weight = np.full((full,), 2.0 / full)
+    weight[0] = weight[rows] = 1.0 / full
+    backward = (forward[:, :rows] * weight[:, None]).T
+    return forward, backward
+
+
+def host_split(table):
+    high = table.astype(jnp.bfloat16)
+    low = (table - high.astype(np.float64)).astype(jnp.bfloat16)
+    return jnp.asarray(high), jnp.asarray(low)
+
+
+def dot(a, b, contract=((1,), (0,))):
+    return lax.dot_general(a, b, (contract, ((), ())), preferred_element_type=jnp.float32)
+
+
+def block_kernel(
+    count,
+    gate_in,
+    value_in,
+    long_in,
+    key_in,
+    val_in,
+    short_in,
+    weight_in,
+    fwd_high_in,
+    fwd_low_in,
+    inv_high_in,
+    inv_low_in,
+    out,
+    held,
+    short_taps,
+    head_weight,
+    fwd_high,
+    fwd_low,
+    inv_high,
+    inv_low,
+    grid_re,
+    grid_im,
+    grid_nyq,
+    sig_re,
+    sig_im,
+    conv,
+    weights,
+    sums,
+    result,
+    send_sem,
+    recv_sem,
+    own_sem,
+    out_send,
+    out_recv,
+    out_own,
+    table_sem,
+):
+    me = lax.axis_index("seq")
+    rows = gate_in.shape[0]
+    width = held.shape[2]
+    heads = width // HEAD_DIM
+    streams = (gate_in, value_in, long_in, key_in, val_in)
+    GATE, VALUE, LONG, KEY, VAL = range(5)
+
+    tables = [
+        pltpu.make_async_copy(source, target, table_sem.at[i])
+        for i, (source, target) in enumerate(
+            (
+                (fwd_high_in, fwd_high),
+                (fwd_low_in, fwd_low),
+                (inv_high_in, inv_high),
+                (inv_low_in, inv_low),
+                (short_in.at[pl.ds(pl.multiple_of(me * width, width), width)], short_taps),
+                (weight_in.at[pl.ds(me * heads, heads)], head_weight),
+            )
+        )
+    ]
+    for copy in tables:
+        copy.start()
+    my_rows = pl.ds(pl.multiple_of(me * rows, rows), rows)
+    my_columns = pl.ds(pl.multiple_of(me * width, width), width)
+    own = [
+        pltpu.make_async_copy(stream.at[:, my_columns], held.at[a, my_rows], own_sem.at[a])
+        for a, stream in enumerate(streams)
+    ]
+    for copy in own:
+        copy.start()
+
+    barrier = pltpu.get_barrier_semaphore()
+    for step in range(1, count):
+        peer = lax.rem(me + step, count)
+        pl.semaphore_signal(
+            barrier, inc=1, device_id={"seq": peer}, device_id_type=pl.DeviceIdType.MESH
+        )
+    pl.semaphore_wait(barrier, count - 1)
+
+    def exchange(a, step):
+        peer = lax.rem(me + step, count)
+        peer_columns = pl.ds(pl.multiple_of(peer * width, width), width)
+        return pltpu.make_async_remote_copy(
+            src_ref=streams[a].at[:, peer_columns],
+            dst_ref=held.at[a, my_rows],
+            send_sem=send_sem.at[a, peer],
+            recv_sem=recv_sem.at[a, me],
+            device_id={"seq": peer},
+            device_id_type=pl.DeviceIdType.MESH,
+        )
+
+    sent = [exchange(a, step) for a in range(5) for step in range(1, count)]
+    for copy in sent:
+        copy.start()
+
+    def arrive(a):
+        own[a].wait()
+        for step in range(1, count):
+            peer = lax.rem(me + step, count)
+            peer_rows = pl.ds(pl.multiple_of(peer * rows, rows), rows)
+            pltpu.make_async_remote_copy(
+                src_ref=streams[a].at[:, my_columns],
+                dst_ref=held.at[a, peer_rows],
+                send_sem=send_sem.at[a, peer],
+                recv_sem=recv_sem.at[a, peer],
+                device_id={"seq": peer},
+                device_id_type=pl.DeviceIdType.MESH,
+            ).wait_recv()
+
+    for copy in tables:
+        copy.wait()
+
+    def forward(signal):
+        depth = signal.shape[0]
+        both = dot(fwd_high[:, :depth], signal) + dot(fwd_low[:, :depth], signal)
+        return both[:rows], both[rows:]
+
+    def backward(re, im):
+        re_high, re_low = split_pair(re)
+        im_high, im_low = split_pair(im)
+        high = jnp.concatenate([re_high, im_high], axis=0)
+        low = jnp.concatenate([re_low, im_low], axis=0)
+        return dot(inv_high[...], high) + (dot(inv_low[...], high) + dot(inv_high[...], low))
+
+    def factor_parts(re, im):
+        first = lax.broadcasted_iota(jnp.int32, re.shape, 0) == 0
+        return re, jnp.where(first, 0.0, im), jnp.where(first, im, re)
+
+    def window(a, block):
+        now = held[a, block * rows : (block + 1) * rows]
+        if block == 0:
+            return now
+        return jnp.concatenate([now, held[a, (block - 1) * rows : block * rows]], axis=0)
+
+    taps_high, taps_low = split_pair(short_taps[...])
+    last = ((1,), (1,))
+    taps_both = dot(fwd_high[:, :TAPS], taps_high, last) + (
+        dot(fwd_low[:, :TAPS], taps_high, last) + dot(fwd_high[:, :TAPS], taps_low, last)
+    )
+    taps_re, taps_im, taps_nyq = factor_parts(taps_both[:rows], taps_both[rows:])
+
+    arrive(GATE)
+    arrive(VALUE)
+    for block in range(count):
+        re, im = forward(window(GATE, block))
+        smoothed = backward(re * taps_re - im * taps_im, re * taps_im + im * taps_nyq)
+        mixed = (
+            smoothed * held[VALUE, block * rows : (block + 1) * rows].astype(jnp.float32)
+        ).astype(jnp.bfloat16)
+        re, im = forward(mixed)
+        sig_re[block], sig_im[block] = re, im
+
+    arrive(LONG)
+    for block in range(count):
+        re, im, nyq = factor_parts(*forward(window(LONG, block)))
+        grid_re[block], grid_im[block], grid_nyq[block] = re, im, nyq
+    for block in range(count):
+        re = im = None
+        for source in range(block + 1):
+            lag = block - source
+            s_re, s_im = sig_re[source], sig_im[source]
+            re_term = s_re * grid_re[lag] - s_im * grid_im[lag]
+            im_term = s_re * grid_im[lag] + s_im * grid_nyq[lag]
+            re = re_term if re is None else re + re_term
+            im = im_term if im is None else im + im_term
+        conv[block * rows : (block + 1) * rows] = backward(re, im).astype(jnp.bfloat16)
+
+    arrive(KEY)
+    scale = 1.0 / math.sqrt(HEAD_DIM)
+    for head in range(heads):
+        columns = slice(head * HEAD_DIM, (head + 1) * HEAD_DIM)
+        for block in range(count):
+            here = slice(block * rows, (block + 1) * rows)
+            past = (block + 1) * rows
+            query = dot(conv[here, columns], head_weight[head]).astype(jnp.bfloat16)
+            scores = dot(query, held[KEY, :past, columns], last) * scale
+            key_pos = lax.broadcasted_iota(jnp.int32, scores.shape, 1)
+            query_pos = block * rows + lax.broadcasted_iota(jnp.int32, scores.shape, 0)
+            allowed = key_pos <= query_pos
+            scores = jnp.where(allowed, scores, -1e30)
+            peak = jnp.max(scores, axis=1, keepdims=True)
+            share = jnp.where(allowed, jnp.exp(scores - peak), 0.0)
+            sums[head, here] = jnp.broadcast_to(
+                jnp.sum(share, axis=1, keepdims=True), (rows, HEAD_DIM)
+            )
+            weights[head, here, :past] = share.astype(jnp.bfloat16)
+
+    arrive(VAL)
+
+    def give_back(block, head, peer):
+        columns = pl.ds(pl.multiple_of(me * width + head * HEAD_DIM, HEAD_DIM), HEAD_DIM)
+        return pltpu.make_async_remote_copy(
+            src_ref=result.at[head, block * rows : (block + 1) * rows],
+            dst_ref=out.at[:, columns],
+            send_sem=out_send.at[block, head],
+            recv_sem=out_recv.at[me, head],
+            device_id={"seq": peer},
+            device_id_type=pl.DeviceIdType.MESH,
+        )
+
+    def keep(block, head):
+        columns = pl.ds(pl.multiple_of(me * width + head * HEAD_DIM, HEAD_DIM), HEAD_DIM)
+        return pltpu.make_async_copy(
+            result.at[head, block * rows : (block + 1) * rows], out.at[:, columns], out_own.at[head]
+        )
+
+    for head in range(heads):
+        for block in reversed(range(count)):
+            here = slice(block * rows, (block + 1) * rows)
+            past = (block + 1) * rows
+            columns = slice(head * HEAD_DIM, (head + 1) * HEAD_DIM)
+            product = dot(weights[head, here, :past], held[VAL, :past, columns])
+            result[head, here] = (product / sums[head, here]).astype(jnp.bfloat16)
+
+            @pl.when(me != block)
+            def _():
+                give_back(block, head, block).start()
+
+            @pl.when(me == block)
+            def _():
+                keep(block, head).start()
+
+    for copy in sent:
+        copy.wait_send()
+    for head in range(heads):
+        for step in range(1, count):
+            peer = lax.rem(me + step, count)
+            columns = pl.ds(pl.multiple_of(peer * width + head * HEAD_DIM, HEAD_DIM), HEAD_DIM)
+            pltpu.make_async_remote_copy(
+                src_ref=result.at[head, :rows],
+                dst_ref=out.at[:, columns],
+                send_sem=out_send.at[0, head],
+                recv_sem=out_recv.at[peer, head],
+                device_id={"seq": peer},
+                device_id_type=pl.DeviceIdType.MESH,
+            ).wait_recv()
+        for block in range(count):
+
+            @pl.when(me != block)
+            def _():
+                give_back(block, head, block).wait_send()
+
+            @pl.when(me == block)
+            def _():
+                keep(block, head).wait()
+
+
+def head_shards(
+    count, gate_input, value_input, short_filter, long_filter, query_weight, key_matrix, value_matrix
+):
+    rows, local_width = gate_input.shape
+    width = local_width // count
+    heads = width // HEAD_DIM
+    length = count * rows
+    forward, inverse_table = transform_tables(rows)
+    forward = host_split(forward)
+    inverse_table = host_split(inverse_table)
+    bf16, f32 = jnp.bfloat16, jnp.float32
+    return pl.pallas_call(
+        functools.partial(block_kernel, count),
+        out_shape=jax.ShapeDtypeStruct((rows, local_width), bf16),
+        in_specs=[pl.BlockSpec(memory_space=pl.ANY)] * 11,
+        out_specs=pl.BlockSpec(memory_space=pl.ANY),
+        scratch_shapes=[
+            pltpu.VMEM((5, length, width), bf16),
+            pltpu.VMEM((width, TAPS), f32),
+            pltpu.VMEM((heads, HEAD_DIM, HEAD_DIM), bf16),
+            pltpu.VMEM((2 * rows, 2 * rows), bf16),
+            pltpu.VMEM((2 * rows, 2 * rows), bf16),
+            pltpu.VMEM((rows, 2 * rows), bf16),
+            pltpu.VMEM((rows, 2 * rows), bf16),
+            pltpu.VMEM((count, rows, width), f32),
+            pltpu.VMEM((count, rows, width), f32),
+            pltpu.VMEM((count, rows, width), f32),
+            pltpu.VMEM((count, rows, width), f32),
+            pltpu.VMEM((count, rows, width), f32),
+            pltpu.VMEM((length, width), bf16),
+            pltpu.VMEM((heads, length, length), bf16),
+            pltpu.VMEM((heads, length, HEAD_DIM), f32),
+            pltpu.VMEM((heads, length, HEAD_DIM), bf16),
+            pltpu.SemaphoreType.DMA((5, count)),
+            pltpu.SemaphoreType.DMA((5, count)),
+            pltpu.SemaphoreType.DMA((5,)),
+            pltpu.SemaphoreType.DMA((count, heads)),
+            pltpu.SemaphoreType.DMA((count, heads)),
+            pltpu.SemaphoreType.DMA((heads,)),
+            pltpu.SemaphoreType.DMA((6,)),
+        ],
+        compiler_params=pltpu.CompilerParams(collective_id=0, has_side_effects=True),
+    )(
+        gate_input,
+        value_input,
+        long_filter,
+        key_matrix,
+        value_matrix,
+        short_filter,
+        query_weight,
+        *forward,
+        *inverse_table,
+    )
+
+
+def shards(count, gate_input, *others):
+    rows, local_width = gate_input.shape
+    by_heads = local_width % (count * HEAD_DIM) == 0 and rows >= TAPS and rows % HEAD_DIM == 0
+    if count > 1 and by_heads:
+        return head_shards(count, gate_input, *others)
+    return general_shards(gate_input, *others)
+
+
 def solution(mesh):
     in_specs = (
         P(("groups", "seq"), "chan"),
@@ -204,4 +543,5 @@
         P(("groups", "seq"), "chan"),
     )
     out_specs = P(("groups", "seq"), "chan")
-    return jax.shard_map(shards, mesh=mesh, in_specs=in_specs, out_specs=out_specs, check_vma=False)
+    return jax.shard_map(
+        functools.partial(shards, mesh.shape["seq"]), mesh=mesh, in_specs=in_specs, out_specs=out_specs, check_vma=False)

time: 74.3 us -> 26.8 us (0.36)
  Pallas kernels: 0 us -> 25 us
  matrix products: 19.4 us -> 0 us
  between operations: 13.7 us -> 0.01 us
  starting transfers between devices: 13.4 us -> 0 us
  waiting for transfers between devices: 10.8 us -> 0 us
  local copies, waits for them, and re-layouts: 10.8 us -> 1.67 us
  other arithmetic: 5.68 us -> 0 us
    pallas_call x0 -> x1, Pallas kernels: none -> 25 us  [head_shards(): pl.pallas_call(functools.partial(block_kernel, count), out_shape=jax.Shap...]
    dot_general x9 -> x0, matrix products: 13.8 us -> none  [the longest x2 5.23 us: spectrum(): jnp.einsum('ckn,nm->ckm', joined, block_table(factor, -1.0), precision=HI...]
    all_to_all x3 -> x0, starting transfers between devices: 10.8 us -> none  [the longest x1 3.85 us: shards(): lax.all_to_all(long_filter.T, 'seq', split_axis=0, concat_axis=1, tiled=T...]
    all_to_all x3 -> x0, waiting for transfers between devices: 10.7 us -> none  [the longest x1 5.91 us: shards(): lax.all_to_all(conv_line, 'seq', split_axis=1, concat_axis=0, tiled=True)]
    conv_general_dilated x1 -> x0, matrix products: 5.61 us -> none  [shards(): lax.conv_general_dilated(padded[None], kernel, (1,), 'VALID', dimension_n...]
    unnamed x13 -> x1, local copies, waits for them, and re-layouts: 4.55 us -> 1.67 us
    ppermute x1 -> x0, starting transfers between devices: 2.54 us -> none  [shifted(): lax.ppermute(value, axis, [(source, source + steps) for source in range(i...]
    concatenate x1 -> x0, local copies, waits for them, and re-layouts: 2.47 us -> none  [shards(): jnp.concatenate([signal_re * kernel_re - signal_im * kernel_im, signal_re...]
  transfers between devices with their start and end apart: 6 -> 0, of which waited for: 2 -> 0; matrix products, arithmetic and copies ran while one was open for 40% -> 0% of each run, Pallas kernels for 0% -> 0%
where the time goes in v1:
time: 26.8 us; the launch traced here: 26.7 us
  Pallas kernels  25 us (93%)
  local copies, waits for them, and re-layouts  1.67 us (6%)
    pallas_call x1, Pallas kernels, head_shards(): pl.pallas_call(functools.partial(block_kernel, count), out_shape=jax.Shap...  25 us
    unnamed x1, local copies, waits for them, and re-layouts  1.67 us

profile of v1, /device:TPU:0, one launch (start us, length us, event | category | flops | bytes accessed | tf_op | source)
XLA Modules:
  0.0 26.7 jit_solution(5956501332599397313)
XLA Ops:
  0.0 25.0 %shard_map.109 = bf16[128,1024]{1,0:T(8,128)(2,1)} custom-call(bf16[128,1024]{1,0:T(8,128)(2,1)} %gate_in.1, bf16[128,1024]{1,0:T(8,128)(2,1)} %value_in.1, bf16[128,1024]{1,0:T(8,128)(2,1)} %long_in.1, bf16[128,1024]{1,0:T(8,128)(2,1)} %key_in.1, bf16[128,1024]{1,0:T(8,128)(2,1)} %val_in.1, f32[1024,128]{1,0:T(8,128)} %short_in.1, ...), custom_call_target="tpu_custom_call" | custom-call | tf_op jit(solution)/shard_map/pallas_call | solution.py:483
  25.0 1.7 %copy.13 = bf16[128,1024]{1,0:T(8,128)(2,1)} copy(bf16[128,1024]{1,0:T(8,128)(2,1)} %shard_map.109) | data formatting | bytes 524288

commit v2 on v1

--- a/solution.py
+++ b/solution.py
@@ -254,6 +254,9 @@
     weights,
     sums,
     result,
+    smoothed,
+    pass_send,
+    pass_recv,
     send_sem,
     recv_sem,
     own_sem,
@@ -268,6 +271,19 @@
     heads = width // HEAD_DIM
     streams = (gate_in, value_in, long_in, key_in, val_in)
     GATE, VALUE, LONG, KEY, VAL = range(5)
+    groups = lax.axis_size("groups")
+    my_group = lax.axis_index("groups")
+    share = width // groups
+
+    def flip(index):
+        return index + 1 - 2 * lax.rem(index, 2)
+
+    partner = flip(me)
+    far = []
+    for step in range(2, count, 2):
+        other = lax.rem(me + step, count)
+        far += [other, flip(other)]
+    peers = [*far, partner]
 
     tables = [
         pltpu.make_async_copy(source, target, table_sem.at[i])
@@ -294,42 +310,62 @@
         copy.start()
 
     barrier = pltpu.get_barrier_semaphore()
-    for step in range(1, count):
-        peer = lax.rem(me + step, count)
+    siblings = [lax.rem(my_group + step, groups) for step in range(1, groups)]
+    for peer in peers:
         pl.semaphore_signal(
             barrier, inc=1, device_id={"seq": peer}, device_id_type=pl.DeviceIdType.MESH
         )
-    pl.semaphore_wait(barrier, count - 1)
-
-    def exchange(a, step):
-        peer = lax.rem(me + step, count)
-        peer_columns = pl.ds(pl.multiple_of(peer * width, width), width)
+    for sibling in siblings:
+        pl.semaphore_signal(
+            barrier, inc=1, device_id={"groups": sibling}, device_id_type=pl.DeviceIdType.MESH
+        )
+    pl.semaphore_wait(barrier, len(peers) + len(siblings))
+
+    def block_of(index):
+        return pl.ds(pl.multiple_of(index * rows, rows), rows)
+
+    def exchange(a, slot, peer, source, first, breadth):
+        there = pl.ds(pl.multiple_of(peer * width + first, HEAD_DIM), breadth)
+        here = pl.ds(pl.multiple_of(first, HEAD_DIM), breadth)
         return pltpu.make_async_remote_copy(
-            src_ref=streams[a].at[:, peer_columns],
-            dst_ref=held.at[a, my_rows],
-            send_sem=send_sem.at[a, peer],
-            recv_sem=recv_sem.at[a, me],
+            src_ref=streams[a].at[:, there],
+            dst_ref=held.at[a, block_of(source), here],
+            send_sem=send_sem.at[slot, peer],
+            recv_sem=recv_sem.at[slot, source],
             device_id={"seq": peer},
             device_id_type=pl.DeviceIdType.MESH,
         )
 
-    sent = [exchange(a, step) for a in range(5) for step in range(1, count)]
+    def pass_on(step, source):
+        here = pl.ds(pl.multiple_of(my_group * share, HEAD_DIM), share)
+        return pltpu.make_async_remote_copy(
+            src_ref=held.at[LONG, block_of(source), here],
+            dst_ref=held.at[LONG, block_of(source), here],
+            send_sem=pass_send.at[step, source],
+            recv_sem=pass_recv.at[step, source],
+            device_id={"groups": siblings[step]},
+            device_id_type=pl.DeviceIdType.MESH,
+        )
+
+    def long_part(peer):
+        return (0, width) if peer is partner else (my_group * share, share)
+
+    sent = []
+    for peer in peers:
+        sent.append(exchange(LONG, 0, peer, me, *long_part(peer)))
+    for a, slot in ((GATE, 1), (VALUE, 2)):
+        for peer in peers:
+            sent.append(exchange(a, slot, peer, me, 0, width))
+    for head in range(heads):
+        for a, slot in ((KEY, 3 + 2 * head), (VAL, 4 + 2 * head)):
+            for peer in peers:
+                sent.append(exchange(a, slot, peer, me, head * HEAD_DIM, HEAD_DIM))
     for copy in sent:
         copy.start()
 
-    def arrive(a):
-        own[a].wait()
-        for step in range(1, count):
-            peer = lax.rem(me + step, count)
-            peer_rows = pl.ds(pl.multiple_of(peer * rows, rows), rows)
-            pltpu.make_async_remote_copy(
-                src_ref=streams[a].at[:, my_columns],
-                dst_ref=held.at[a, peer_rows],
-                send_sem=send_sem.at[a, peer],
-                recv_sem=recv_sem.at[a, peer],
-                device_id={"seq": peer},
-                device_id_type=pl.DeviceIdType.MESH,
-            ).wait_recv()
+    def arrive(a, slot, first=0, breadth=width):
+        for peer in peers:
+            exchange(a, slot, peer, peer, first, breadth).wait_recv()
 
     for copy in tables:
         copy.wait()
@@ -363,21 +399,34 @@
     )
     taps_re, taps_im, taps_nyq = factor_parts(taps_both[:rows], taps_both[rows:])
 
-    arrive(GATE)
-    arrive(VALUE)
+    passed = []
+    for peer in peers:
+        exchange(LONG, 0, peer, peer, *long_part(peer)).wait_recv()
+        if peer is not partner:
+            for step in range(groups - 1):
+                passed.append(pass_on(step, peer))
+                passed[-1].start()
+
+    own[GATE].wait()
+    arrive(GATE, 1)
     for block in range(count):
         re, im = forward(window(GATE, block))
-        smoothed = backward(re * taps_re - im * taps_im, re * taps_im + im * taps_nyq)
-        mixed = (
-            smoothed * held[VALUE, block * rows : (block + 1) * rows].astype(jnp.float32)
-        ).astype(jnp.bfloat16)
-        re, im = forward(mixed)
-        sig_re[block], sig_im[block] = re, im
-
-    arrive(LONG)
+        smoothed[block] = backward(re * taps_re - im * taps_im, re * taps_im + im * taps_nyq)
+
+    own[LONG].wait()
+    for copy in passed:
+        copy.wait_recv()
     for block in range(count):
         re, im, nyq = factor_parts(*forward(window(LONG, block)))
         grid_re[block], grid_im[block], grid_nyq[block] = re, im, nyq
+
+    own[VALUE].wait()
+    arrive(VALUE, 2)
+    for block in range(count):
+        here = slice(block * rows, (block + 1) * rows)
+        mixed = (smoothed[block] * held[VALUE, here].astype(jnp.float32)).astype(jnp.bfloat16)
+        sig_re[block], sig_im[block] = forward(mixed)
+
     for block in range(count):
         re = im = None
         for source in range(block + 1):
@@ -389,9 +438,28 @@
             im = im_term if im is None else im + im_term
         conv[block * rows : (block + 1) * rows] = backward(re, im).astype(jnp.bfloat16)
 
-    arrive(KEY)
+    def give_back(block, head, peer):
+        columns = pl.ds(pl.multiple_of(me * width + head * HEAD_DIM, HEAD_DIM), HEAD_DIM)
+        return pltpu.make_async_remote_copy(
+            src_ref=result.at[head, block * rows : (block + 1) * rows],
+            dst_ref=out.at[:, columns],
+            send_sem=out_send.at[block, head],
+            recv_sem=out_recv.at[me, head],
+            device_id={"seq": peer},
+            device_id_type=pl.DeviceIdType.MESH,
+        )
+
+    def keep(block, head):
+        columns = pl.ds(pl.multiple_of(me * width + head * HEAD_DIM, HEAD_DIM), HEAD_DIM)
+        return pltpu.make_async_copy(
+            result.at[head, block * rows : (block + 1) * rows], out.at[:, columns], out_own.at[head]
+        )
+
     scale = 1.0 / math.sqrt(HEAD_DIM)
+    own[KEY].wait()
+    own[VAL].wait()
     for head in range(heads):
+        arrive(KEY, 3 + 2 * head, head * HEAD_DIM, HEAD_DIM)
         columns = slice(head * HEAD_DIM, (head + 1) * HEAD_DIM)
         for block in range(count):
             here = slice(block * rows, (block + 1) * rows)
@@ -409,26 +477,7 @@
             )
             weights[head, here, :past] = share.astype(jnp.bfloat16)
 
-    arrive(VAL)
-
-    def give_back(block, head, peer):
-        columns = pl.ds(pl.multiple_of(me * width + head * HEAD_DIM, HEAD_DIM), HEAD_DIM)
-        return pltpu.make_async_remote_copy(
-            src_ref=result.at[head, block * rows : (block + 1) * rows],
-            dst_ref=out.at[:, columns],
-            send_sem=out_send.at[block, head],
-            recv_sem=out_recv.at[me, head],
-            device_id={"seq": peer},
-            device_id_type=pl.DeviceIdType.MESH,
-        )
-
-    def keep(block, head):
-        columns = pl.ds(pl.multiple_of(me * width + head * HEAD_DIM, HEAD_DIM), HEAD_DIM)
-        return pltpu.make_async_copy(
-            result.at[head, block * rows : (block + 1) * rows], out.at[:, columns], out_own.at[head]
-        )
-
-    for head in range(heads):
+        arrive(VAL, 4 + 2 * head, head * HEAD_DIM, HEAD_DIM)
         for block in reversed(range(count)):
             here = slice(block * rows, (block + 1) * rows)
             past = (block + 1) * rows
@@ -444,11 +493,10 @@
             def _():
                 keep(block, head).start()
 
-    for copy in sent:
+    for copy in [*sent, *passed]:
         copy.wait_send()
     for head in range(heads):
-        for step in range(1, count):
-            peer = lax.rem(me + step, count)
+        for peer in peers:
             columns = pl.ds(pl.multiple_of(peer * width + head * HEAD_DIM, HEAD_DIM), HEAD_DIM)
             pltpu.make_async_remote_copy(
                 src_ref=result.at[head, :rows],
@@ -470,7 +518,15 @@
 
 
 def head_shards(
-    count, gate_input, value_input, short_filter, long_filter, query_weight, key_matrix, value_matrix
+    count,
+    groups,
+    gate_input,
+    value_input,
+    short_filter,
+    long_filter,
+    query_weight,
+    key_matrix,
+    value_matrix,
 ):
     rows, local_width = gate_input.shape
     width = local_width // count
@@ -482,9 +538,9 @@
     bf16, f32 = jnp.bfloat16, jnp.float32
     return pl.pallas_call(
         functools.partial(block_kernel, count),
-        out_shape=jax.ShapeDtypeStruct((rows, local_width), bf16),
+        out_shape=pltpu.VMEM((rows, local_width), bf16),
         in_specs=[pl.BlockSpec(memory_space=pl.ANY)] * 11,
-        out_specs=pl.BlockSpec(memory_space=pl.ANY),
+        out_specs=pl.BlockSpec(memory_space=pltpu.VMEM),
         scratch_shapes=[
             pltpu.VMEM((5, length, width), bf16),
             pltpu.VMEM((width, TAPS), f32),
@@ -502,8 +558,11 @@
             pltpu.VMEM((heads, length, length), bf16),
             pltpu.VMEM((heads, length, HEAD_DIM), f32),
             pltpu.VMEM((heads, length, HEAD_DIM), bf16),
-            pltpu.SemaphoreType.DMA((5, count)),
-            pltpu.SemaphoreType.DMA((5, count)),
+            pltpu.VMEM((count, rows, width), f32),
+            pltpu.SemaphoreType.DMA((groups - 1, count)),
+            pltpu.SemaphoreType.DMA((groups - 1, count)),
+            pltpu.SemaphoreType.DMA((3 + 2 * heads, count)),
+            pltpu.SemaphoreType.DMA((3 + 2 * heads, count)),
             pltpu.SemaphoreType.DMA((5,)),
             pltpu.SemaphoreType.DMA((count, heads)),
             pltpu.SemaphoreType.DMA((count, heads)),
@@ -524,11 +583,12 @@
     )
 
 
-def shards(count, gate_input, *others):
+def shards(count, groups, gate_input, *others):
     rows, local_width = gate_input.shape
-    by_heads = local_width % (count * HEAD_DIM) == 0 and rows >= TAPS and rows % HEAD_DIM == 0
-    if count > 1 and by_heads:
-        return head_shards(count, gate_input, *others)
+    by_heads = local_width % (count * groups * HEAD_DIM) == 0
+    by_rows = rows >= TAPS and rows % HEAD_DIM == 0
+    if count % 2 == 0 and groups > 1 and by_heads and by_rows:
+        return head_shards(count, groups, gate_input, *others)
     return general_shards(gate_input, *others)
 
 
@@ -544,4 +604,4 @@
     )
     out_specs = P(("groups", "seq"), "chan")
     return jax.shard_map(
-        functools.partial(shards, mesh.shape["seq"]), mesh=mesh, in_specs=in_specs, out_specs=out_specs, check_vma=False)
+        functools.partial(shards, mesh.shape["seq"], mesh.shape["groups"]), mesh=mesh, in_specs=in_specs, out_specs=out_specs, check_vma=False)

time: 26.8 us -> 23.3 us (0.87)
  Pallas kernels: 25 us -> 22.5 us
  local copies, waits for them, and re-layouts: 1.67 us -> 0.71 us
    pallas_call x1, Pallas kernels: 25 us -> 22.5 us  [head_shards(): pl.pallas_call(functools.partial(block_kernel, count), out_shape=pltpu.VM...]
    unnamed x1, local copies, waits for them, and re-layouts: 1.67 us -> 0.71 us
where the time goes in v2:
time: 23.3 us; the launch traced here: 23.2 us
  Pallas kernels  22.5 us (97%)
  local copies, waits for them, and re-layouts  0.71 us (3%)
    pallas_call x1, Pallas kernels, head_shards(): pl.pallas_call(functools.partial(block_kernel, count), out_shape=pltpu.VM...  22.5 us
    unnamed x1, local copies, waits for them, and re-layouts  0.71 us

profile of v2, /device:TPU:0, one launch (start us, length us, event | category | flops | bytes accessed | tf_op | source)
XLA Modules:
  0.0 23.2 jit_solution(3841473878208838434)
XLA Ops:
  0.0 22.5 %shard_map.109 = bf16[128,1024]{1,0:T(8,128)(2,1)S(1)} custom-call(bf16[128,1024]{1,0:T(8,128)(2,1)} %gate_in.1, bf16[128,1024]{1,0:T(8,128)(2,1)} %value_in.1, bf16[128,1024]{1,0:T(8,128)(2,1)} %long_in.1, bf16[128,1024]{1,0:T(8,128)(2,1)} %key_in.1, bf16[128,1024]{1,0:T(8,128)(2,1)} %val_in.1, f32[1024,128]{1,0:T(8,128)} %short_in.1, ...), custom_call_target="tpu_custom_call" | custom-call | tf_op jit(solution)/shard_map/pallas_call | solution.py:539
  22.5 0.7 %copy.13 = bf16[128,1024]{1,0:T(8,128)(2,1)} copy(bf16[128,1024]{1,0:T(8,128)(2,1)S(1)} %shard_map.109) | data formatting | bytes 524288

commit v3 on v2

--- a/solution.py
+++ b/solution.py
@@ -255,6 +255,13 @@
     sums,
     result,
     smoothed,
+    mixed,
+    far_taps,
+    far_gate,
+    far_before,
+    far_value,
+    far_mixed,
+    halo_sem,
     pass_send,
     pass_recv,
     send_sem,
@@ -279,11 +286,11 @@
         return index + 1 - 2 * lax.rem(index, 2)
 
     partner = flip(me)
-    far = []
-    for step in range(2, count, 2):
-        other = lax.rem(me + step, count)
-        far += [other, flip(other)]
+    opposite = lax.rem(me + 2, count)
+    far = [opposite, flip(opposite)]
     peers = [*far, partner]
+    late = me // 2
+    far_columns = pl.ds(pl.multiple_of((1 - late) * 2 * width, 2 * width), 2 * width)
 
     tables = [
         pltpu.make_async_copy(source, target, table_sem.at[i])
@@ -294,6 +301,9 @@
                 (inv_high_in, inv_high),
                 (inv_low_in, inv_low),
                 (short_in.at[pl.ds(pl.multiple_of(me * width, width), width)], short_taps),
+                (short_in.at[far_columns], far_taps),
+                (gate_in.at[:, far_columns], far_gate),
+                (value_in.at[:, far_columns], far_value),
                 (weight_in.at[pl.ds(me * heads, heads)], head_weight),
             )
         )
@@ -350,18 +360,52 @@
     def long_part(peer):
         return (0, width) if peer is partner else (my_group * share, share)
 
+    halo = pltpu.make_async_remote_copy(
+        src_ref=gate_in.at[:, far_columns],
+        dst_ref=far_before,
+        send_sem=halo_sem.at[0],
+        recv_sem=halo_sem.at[1],
+        device_id={"seq": partner},
+        device_id_type=pl.DeviceIdType.MESH,
+    )
+
+    def send_mixed(peer, source):
+        there = pl.ds(pl.multiple_of(lax.rem(peer, 2) * width, width), width)
+        return pltpu.make_async_remote_copy(
+            src_ref=far_mixed.at[:, there],
+            dst_ref=mixed.at[block_of(source)],
+            send_sem=send_sem.at[3, peer],
+            recv_sem=recv_sem.at[3, source],
+            device_id={"seq": peer},
+            device_id_type=pl.DeviceIdType.MESH,
+        )
+
+    @pl.when(lax.rem(me, 2) == 0)
+    def _():
+        halo.start()
+
     sent = []
     for peer in peers:
         sent.append(exchange(LONG, 0, peer, me, *long_part(peer)))
     for a, slot in ((GATE, 1), (VALUE, 2)):
-        for peer in peers:
-            sent.append(exchange(a, slot, peer, me, 0, width))
-    for head in range(heads):
-        for a, slot in ((KEY, 3 + 2 * head), (VAL, 4 + 2 * head)):
-            for peer in peers:
-                sent.append(exchange(a, slot, peer, me, head * HEAD_DIM, HEAD_DIM))
+        sent.append(exchange(a, slot, partner, me, 0, width))
     for copy in sent:
         copy.start()
+    raw_gate = [exchange(GATE, 1, peer, me, 0, width) for peer in far]
+    raw_value = [exchange(VALUE, 2, peer, me, 0, width) for peer in far]
+    sent_mixed = [send_mixed(peer, me) for peer in far]
+    sends_gate = jnp.logical_or(me == 1, me == 2)
+    sends_value = me == 2
+
+    @pl.when(sends_gate)
+    def _():
+        for copy in raw_gate:
+            copy.start()
+
+    @pl.when(sends_value)
+    def _():
+        for copy in raw_value:
+            copy.start()
 
     def arrive(a, slot, first=0, breadth=width):
         for peer in peers:
@@ -392,12 +436,44 @@
             return now
         return jnp.concatenate([now, held[a, (block - 1) * rows : block * rows]], axis=0)
 
-    taps_high, taps_low = split_pair(short_taps[...])
     last = ((1,), (1,))
-    taps_both = dot(fwd_high[:, :TAPS], taps_high, last) + (
-        dot(fwd_low[:, :TAPS], taps_high, last) + dot(fwd_high[:, :TAPS], taps_low, last)
-    )
-    taps_re, taps_im, taps_nyq = factor_parts(taps_both[:rows], taps_both[rows:])
+
+    def taps_parts(taps):
+        high, low = split_pair(taps[...])
+        both = dot(fwd_high[:, :TAPS], high, last) + (
+            dot(fwd_low[:, :TAPS], high, last) + dot(fwd_high[:, :TAPS], low, last)
+        )
+        return factor_parts(both[:rows], both[rows:])
+
+    def smooth(signal, parts):
+        re, im = forward(signal)
+        re_part, im_part, nyq_part = parts
+        return backward(re * re_part - im * im_part, re * im_part + im * nyq_part)
+
+    @pl.when(me == 0)
+    def _():
+        far_before[...] = jnp.zeros_like(far_before)
+
+    @pl.when(jnp.logical_not(sends_value))
+    def _():
+        far_parts = taps_parts(far_taps)
+
+        @pl.when(lax.rem(me, 2) == 1)
+        def _():
+            halo.wait_recv()
+
+        filtered = smooth(jnp.concatenate([far_gate[...], far_before[...]], axis=0), far_parts)
+        far_mixed[...] = (filtered * far_value[...].astype(jnp.float32)).astype(jnp.bfloat16)
+        for copy in sent_mixed:
+            copy.start()
+
+    late_sent = []
+    for head in range(heads):
+        for a, slot in ((KEY, 4 + 2 * head), (VAL, 5 + 2 * head)):
+            for peer in peers:
+                late_sent.append(exchange(a, slot, peer, me, head * HEAD_DIM, HEAD_DIM))
+    for copy in late_sent:
+        copy.start()
 
     passed = []
     for peer in peers:
@@ -407,11 +483,31 @@
                 passed.append(pass_on(step, peer))
                 passed[-1].start()
 
+    parts = taps_parts(short_taps)
     own[GATE].wait()
-    arrive(GATE, 1)
-    for block in range(count):
-        re, im = forward(window(GATE, block))
-        smoothed[block] = backward(re * taps_re - im * taps_im, re * taps_im + im * taps_nyq)
+    for source in (partner, 2 - late):
+        exchange(GATE, 1, source, source, 0, width).wait_recv()
+
+    def smooth_blocks(*blocks):
+        for block in blocks:
+            smoothed[block] = smooth(window(GATE, block), parts)
+
+    def mix_blocks(*blocks):
+        for block in blocks:
+            here = slice(block * rows, (block + 1) * rows)
+            mixed[here] = (smoothed[block] * held[VALUE, here].astype(jnp.float32)).astype(
+                jnp.bfloat16
+            )
+
+    smooth_blocks(2)
+
+    @pl.when(late == 0)
+    def _():
+        smooth_blocks(0, 1)
+
+    @pl.when(late == 1)
+    def _():
+        smooth_blocks(3)
 
     own[LONG].wait()
     for copy in passed:
@@ -421,11 +517,22 @@
         grid_re[block], grid_im[block], grid_nyq[block] = re, im, nyq
 
     own[VALUE].wait()
-    arrive(VALUE, 2)
+    exchange(VALUE, 2, partner, partner, 0, width).wait_recv()
+
+    @pl.when(late == 0)
+    def _():
+        exchange(VALUE, 2, 2, 2, 0, width).wait_recv()
+        mix_blocks(0, 1, 2)
+        send_mixed(3, 3).wait_recv()
+
+    @pl.when(late == 1)
+    def _():
+        mix_blocks(2, 3)
+        send_mixed(0, 0).wait_recv()
+        send_mixed(1, 1).wait_recv()
+
     for block in range(count):
-        here = slice(block * rows, (block + 1) * rows)
-        mixed = (smoothed[block] * held[VALUE, here].astype(jnp.float32)).astype(jnp.bfloat16)
-        sig_re[block], sig_im[block] = forward(mixed)
+        sig_re[block], sig_im[block] = forward(mixed[block * rows : (block + 1) * rows])
 
     for block in range(count):
         re = im = None
@@ -459,7 +566,7 @@
     own[KEY].wait()
     own[VAL].wait()
     for head in range(heads):
-        arrive(KEY, 3 + 2 * head, head * HEAD_DIM, HEAD_DIM)
+        arrive(KEY, 4 + 2 * head, head * HEAD_DIM, HEAD_DIM)
         columns = slice(head * HEAD_DIM, (head + 1) * HEAD_DIM)
         for block in range(count):
             here = slice(block * rows, (block + 1) * rows)
@@ -477,7 +584,7 @@
             )
             weights[head, here, :past] = share.astype(jnp.bfloat16)
 
-        arrive(VAL, 4 + 2 * head, head * HEAD_DIM, HEAD_DIM)
+        arrive(VAL, 5 + 2 * head, head * HEAD_DIM, HEAD_DIM)
         for block in reversed(range(count)):
             here = slice(block * rows, (block + 1) * rows)
             past = (block + 1) * rows
@@ -493,8 +600,28 @@
             def _():
                 keep(block, head).start()
 
-    for copy in [*sent, *passed]:
+    for copy in [*sent, *passed, *late_sent]:
         copy.wait_send()
+
+    @pl.when(lax.rem(me, 2) == 0)
+    def _():
+        halo.wait_send()
+
+    @pl.when(sends_gate)
+    def _():
+        for copy in raw_gate:
+            copy.wait_send()
+
+    @pl.when(sends_value)
+    def _():
+        for copy in raw_value:
+            copy.wait_send()
+
+    @pl.when(jnp.logical_not(sends_value))
+    def _():
+        for copy in sent_mixed:
+            copy.wait_send()
+
     for head in range(heads):
         for peer in peers:
             columns = pl.ds(pl.multiple_of(peer * width + head * HEAD_DIM, HEAD_DIM), HEAD_DIM)
@@ -559,15 +686,22 @@
             pltpu.VMEM((heads, length, HEAD_DIM), f32),
             pltpu.VMEM((heads, length, HEAD_DIM), bf16),
             pltpu.VMEM((count, rows, width), f32),
+            pltpu.VMEM((length, width), bf16),
+            pltpu.VMEM((2 * width, TAPS), f32),
+            pltpu.VMEM((rows, 2 * width), bf16),
+            pltpu.VMEM((rows, 2 * width), bf16),
+            pltpu.VMEM((rows, 2 * width), bf16),
+            pltpu.VMEM((rows, 2 * width), bf16),
+            pltpu.SemaphoreType.DMA((2,)),
             pltpu.SemaphoreType.DMA((groups - 1, count)),
             pltpu.SemaphoreType.DMA((groups - 1, count)),
-            pltpu.SemaphoreType.DMA((3 + 2 * heads, count)),
-            pltpu.SemaphoreType.DMA((3 + 2 * heads, count)),
+            pltpu.SemaphoreType.DMA((4 + 2 * heads, count)),
+            pltpu.SemaphoreType.DMA((4 + 2 * heads, count)),
             pltpu.SemaphoreType.DMA((5,)),
             pltpu.SemaphoreType.DMA((count, heads)),
             pltpu.SemaphoreType.DMA((count, heads)),
             pltpu.SemaphoreType.DMA((heads,)),
-            pltpu.SemaphoreType.DMA((6,)),
+            pltpu.SemaphoreType.DMA((9,)),
         ],
         compiler_params=pltpu.CompilerParams(collective_id=0, has_side_effects=True),
     )(
@@ -587,7 +721,8 @@
     rows, local_width = gate_input.shape
     by_heads = local_width % (count * groups * HEAD_DIM) == 0
     by_rows = rows >= TAPS and rows % HEAD_DIM == 0
-    if count % 2 == 0 and groups > 1 and by_heads and by_rows:
+    two_pairs = count == 4
+    if two_pairs and groups > 1 and by_heads and by_rows:
         return head_shards(count, groups, gate_input, *others)
     return general_shards(gate_input, *others)
 

time: 23.3 us -> 22 us (0.944)
  Pallas kernels: 22.5 us -> 21.2 us
    pallas_call x1, Pallas kernels: 22.5 us -> 21.2 us  [head_shards(): pl.pallas_call(functools.partial(block_kernel, count), out_shape=pltpu.VM...]
where the time goes in v3:
time: 22 us; the launch traced here: 21.9 us
  Pallas kernels  21.2 us (96%)
  local copies, waits for them, and re-layouts  0.71 us (3%)
    pallas_call x1, Pallas kernels, head_shards(): pl.pallas_call(functools.partial(block_kernel, count), out_shape=pltpu.VM...  21.2 us
    unnamed x1, local copies, waits for them, and re-layouts  0.71 us

profile of v3, /device:TPU:0, one launch (start us, length us, event | category | flops | bytes accessed | tf_op | source)
XLA Modules:
  0.0 21.9 jit_solution(3979207292762429365)
XLA Ops:
  0.0 21.2 %shard_map.109 = bf16[128,1024]{1,0:T(8,128)(2,1)S(1)} custom-call(bf16[128,1024]{1,0:T(8,128)(2,1)} %gate_in.1, bf16[128,1024]{1,0:T(8,128)(2,1)} %value_in.1, bf16[128,1024]{1,0:T(8,128)(2,1)} %long_in.1, bf16[128,1024]{1,0:T(8,128)(2,1)} %key_in.1, bf16[128,1024]{1,0:T(8,128)(2,1)} %val_in.1, f32[1024,128]{1,0:T(8,128)} %short_in.1, ...), custom_call_target="tpu_custom_call" | custom-call | tf_op jit(solution)/shard_map/pallas_call | solution.py:666
  21.2 0.7 %copy.13 = bf16[128,1024]{1,0:T(8,128)(2,1)} copy(bf16[128,1024]{1,0:T(8,128)(2,1)S(1)} %shard_map.109) | data formatting | bytes 524288

commit v4 on v3

--- a/solution.py
+++ b/solution.py
@@ -584,8 +584,7 @@
             )
             weights[head, here, :past] = share.astype(jnp.bfloat16)
 
-        arrive(VAL, 5 + 2 * head, head * HEAD_DIM, HEAD_DIM)
-        for block in reversed(range(count)):
+        def finish(block):
             here = slice(block * rows, (block + 1) * rows)
             past = (block + 1) * rows
             columns = slice(head * HEAD_DIM, (head + 1) * HEAD_DIM)
@@ -599,6 +598,29 @@
             @pl.when(me == block)
             def _():
                 keep(block, head).start()
+
+        def value_from(source):
+            exchange(
+                VAL, 5 + 2 * head, source, source, head * HEAD_DIM, HEAD_DIM
+            ).wait_recv()
+
+        value_from(partner)
+
+        @pl.when(late == 0)
+        def _():
+            for block in (2, 3):
+                value_from(block)
+                finish(block)
+            finish(1)
+            finish(0)
+
+        @pl.when(late == 1)
+        def _():
+            for block in (0, 1):
+                value_from(block)
+                finish(block)
+            finish(2)
+            finish(3)
 
     for copy in [*sent, *passed, *late_sent]:
         copy.wait_send()

time: 22 us -> 21.3 us (0.968)
  Pallas kernels: 21.2 us -> 20.5 us
    pallas_call x1, Pallas kernels: 21.2 us -> 20.5 us  [head_shards(): pl.pallas_call(functools.partial(block_kernel, count), out_shape=pltpu.VM...]
where the time goes in v4:
time: 21.3 us; the launch traced here: 21.2 us
  Pallas kernels  20.5 us (96%)
  local copies, waits for them, and re-layouts  0.71 us (3%)
    pallas_call x1, Pallas kernels, head_shards(): pl.pallas_call(functools.partial(block_kernel, count), out_shape=pltpu.VM...  20.5 us
    unnamed x1, local copies, waits for them, and re-layouts  0.71 us

profile of v4, /device:TPU:0, one launch (start us, length us, event | category | flops | bytes accessed | tf_op | source)
XLA Modules:
  0.0 21.2 jit_solution(2383100229592040566)
XLA Ops:
  0.0 20.5 %shard_map.109 = bf16[128,1024]{1,0:T(8,128)(2,1)S(1)} custom-call(bf16[128,1024]{1,0:T(8,128)(2,1)} %gate_in.1, bf16[128,1024]{1,0:T(8,128)(2,1)} %value_in.1, bf16[128,1024]{1,0:T(8,128)(2,1)} %long_in.1, bf16[128,1024]{1,0:T(8,128)(2,1)} %key_in.1, bf16[128,1024]{1,0:T(8,128)(2,1)} %val_in.1, f32[1024,128]{1,0:T(8,128)} %short_in.1, ...), custom_call_target="tpu_custom_call" | custom-call | tf_op jit(solution)/shard_map/pallas_call | solution.py:688
  20.5 0.7 %copy.13 = bf16[128,1024]{1,0:T(8,128)(2,1)} copy(bf16[128,1024]{1,0:T(8,128)(2,1)S(1)} %shard_map.109) | data formatting | bytes 524288
